TPU v7x, 32 devices: a whole 2x2x4 slice. The times are simulated.
32 devices in a mesh: dp: 16 (over z, y, x), tensor: 2 (over core).
Axes of the slice: x: 2, y: 2, z: 4, core: 2. Of those that a mesh axis runs over, the one named last changes fastest.
Arguments:
- tokens: bfloat16 [4, 16, 2048, 1024], P(None, 'dp', None, 'tensor'), may hold values from -40 to 40
- routed: int32 [4, 16, 256], P(None, 'dp'), may hold values from 0 to 2047, as said below
- w_query: bfloat16 [1024, 1024], P('dp', 'tensor'), may hold values from -0.1875 to 0.1875
- w_key: bfloat16 [1024, 1024], P('dp', 'tensor'), may hold values from -0.1875 to 0.1875
- w_value: bfloat16 [1024, 1024], P('dp', 'tensor'), may hold values from -0.1875 to 0.1875
- w_out: bfloat16 [1024, 1024], P('tensor', 'dp'), may hold values from -1 to 1
- w_up: bfloat16 [1024, 4096], P('dp', 'tensor'), may hold values from -0.1875 to 0.1875
- w_down: bfloat16 [4096, 1024], P('tensor', 'dp'), may hold values from -0.09375 to 0.09375
- w_route: bfloat16 [1024], P('dp'), may hold values from -0.09375 to 0.09375
- gain_attn: bfloat16 [1024], P('dp'), may hold values from 0.099609375 to 1.8984375
- gain_mlp: bfloat16 [1024], P('dp'), may hold values from 0.099609375 to 1.8984375
- cotangent: bfloat16 [4, 16, 2048, 1024], P(None, 'dp', None, 'tensor'), may hold values from -6 to 6
Outputs:
- output: bfloat16 [4, 16, 2048, 1024], P(None, 'dp', None, 'tensor')
- input_grad: bfloat16 [4, 16, 2048, 1024], P(None, 'dp', None, 'tensor')
- grad_query: float32 [1024, 1024], P('dp', 'tensor')
- grad_key: float32 [1024, 1024], P('dp', 'tensor')
- grad_value: float32 [1024, 1024], P('dp', 'tensor')
- grad_out: float32 [1024, 1024], P('tensor', 'dp')
- grad_up: float32 [1024, 4096], P('dp', 'tensor')
- grad_down: float32 [4096, 1024], P('tensor', 'dp')
- grad_route: float32 [1024], P('dp')
- grad_gain_attn: float32 [1024], P('dp')
- grad_gain_mlp: float32 [1024], P('dp')
Inputs may be any that keep to these rules, and one draw needn't show every extreme that they name: Each row of routed holds 256 different positions of its sequence in rising order.
All inputs are finite; a program needn't handle non-finite values.
Results may differ from a plain program's by a relative error of at most 0.02.
Values may be sent and summed in bfloat16 or wider, within the bound.
A program may use at most 192 MiB of HBM per device.

v0:
```python
import jax
import jax.numpy as jnp
from jax import lax
from jax.sharding import PartitionSpec as P

HD = 64
eps_norm = 1e-05


def rms_norm(values, gain):
    return values * lax.rsqrt(jnp.mean(values * values, -1, keepdims=True) + eps_norm) * gain


def dense(left, right):
    return jnp.dot(left, right, preferred_element_type=jnp.float32)


def shards(
    tokens,
    routed,
    w_query,
    w_key,
    w_value,
    w_out,
    w_up,
    w_down,
    w_route,
    gain_attn,
    gain_mlp,
    cotangent,
):
    half_width = tokens.shape[3]
    capacity = routed.shape[2]
    offset = lax.axis_index("tensor") * half_width
    width = half_width * lax.axis_size("tensor")
    score_scale = HD ** (-0.5)
    causal = lax.broadcasted_iota(jnp.int32, (capacity, capacity), 0) >= lax.broadcasted_iota(
        jnp.int32, (capacity, capacity), 1
    )

    def sequence_step(gradients, weight_rows, weight_cols, tok_seq, chosen, cot_seq):
        full_query, full_key, full_value, full_up, full_route, full_gain1, full_gain2 = weight_rows
        full_out, full_down = weight_cols
        g_query, g_key, g_value, g_up, g_route, g_gain1, g_gain2, g_out, g_down = gradients
        route_f32 = full_route.astype(jnp.float32)
        gain1_f32 = full_gain1.astype(jnp.float32)
        gain2_f32 = full_gain2.astype(jnp.float32)
        rows_half = jnp.take(tok_seq, chosen, axis=0)
        cot_half = jnp.take(cot_seq, chosen, axis=0)
        routed_rows, cot_rows = (
            lax.all_gather(rows_half, "tensor", axis=1, tiled=True),
            lax.all_gather(cot_half, "tensor", axis=1, tiled=True),
        )
        rows_f32 = routed_rows.astype(jnp.float32)
        rows_half_f32 = rows_half.astype(jnp.float32)
        cot_half_f32 = cot_half.astype(jnp.float32)
        route_logit = dense(routed_rows, full_route)
        route_gate = jax.nn.sigmoid(route_logit)
        normed = rms_norm(rows_f32, gain1_f32).astype(jnp.bfloat16)
        queries = dense(normed, full_query).astype(jnp.bfloat16).reshape(capacity, -1, HD)
        key_rows = dense(normed, full_key).astype(jnp.bfloat16).reshape(capacity, -1, HD)
        value_rows = dense(normed, full_value).astype(jnp.bfloat16).reshape(capacity, -1, HD)
        scores = (
            jnp.einsum("qhd,khd->hqk", queries, key_rows, preferred_element_type=jnp.float32)
            * score_scale
        )
        scores = jnp.where(causal[None], scores, -1e30)
        log_total = jax.nn.logsumexp(scores, axis=-1, keepdims=True)
        probs_low = jnp.exp(scores - log_total).astype(jnp.bfloat16)
        mixed_heads = jnp.einsum(
            "hqk,khd->qhd", probs_low, value_rows, preferred_element_type=jnp.float32
        )
        mixed_heads = mixed_heads.astype(jnp.bfloat16).reshape(capacity, -1)
        attended = lax.psum(dense(mixed_heads, full_out).astype(jnp.bfloat16), "tensor").astype(
            jnp.float32
        )
        hidden = rows_f32 + attended
        normed2 = rms_norm(hidden, gain2_f32).astype(jnp.bfloat16)
        up_proj = dense(normed2, full_up)
        activated = jax.nn.gelu(up_proj).astype(jnp.bfloat16)
        down_out = lax.psum(dense(activated, full_down).astype(jnp.bfloat16), "tensor").astype(
            jnp.float32
        )
        branch = attended + down_out
        branch_half = lax.dynamic_slice_in_dim(branch, offset, half_width, 1)
        d_logit = (
            jnp.sum(cot_rows.astype(jnp.float32) * branch, -1) * route_gate * (1.0 - route_gate)
        )
        new_rows = (rows_half_f32 + route_gate[:, None] * branch_half).astype(jnp.bfloat16)
        out_seq = tok_seq.at[chosen].set(new_rows)
        cot_f32 = cot_rows.astype(jnp.float32)
        d_branch = route_gate[:, None] * cot_f32
        d_down = d_branch.astype(jnp.bfloat16)
        up_again = dense(lax.optimization_barrier(normed2), full_up)
        act_again = jax.nn.gelu(up_again).astype(jnp.bfloat16)
        g_down = g_down + dense(act_again.T, d_down)
        d_act = dense(d_down, full_down.T)
        gelu_value, gelu_back = jax.vjp(jax.nn.gelu, up_again)
        d_upper = gelu_back(d_act)[0].astype(jnp.bfloat16)
        g_up = g_up + dense(normed2.T, d_upper)
        d_normed2 = lax.psum(dense(d_upper, full_up.T).astype(jnp.bfloat16), "tensor").astype(
            jnp.float32
        )
        norm2_value, norm2_back = jax.vjp(rms_norm, hidden, gain2_f32)
        d_hidden, d_gain2 = norm2_back(d_normed2)
        g_gain2 = g_gain2 + d_gain2
        d_attended = (d_branch + d_hidden).astype(jnp.bfloat16)
        g_out = g_out + dense(mixed_heads.T, d_attended)
        d_mixed = dense(d_attended, full_out.T).astype(jnp.bfloat16).reshape(capacity, -1, HD)
        scores_again = (
            jnp.einsum("qhd,khd->hqk", queries, key_rows, preferred_element_type=jnp.float32)
            * score_scale
        )
        scores_again = jnp.where(causal[None], scores_again, -1e30)
        attn_probs = jnp.exp(scores_again - log_total)
        probs_again = attn_probs.astype(jnp.bfloat16)
        d_values = jnp.einsum(
            "hqk,qhd->khd", probs_again, d_mixed, preferred_element_type=jnp.float32
        )
        d_values = d_values.astype(jnp.bfloat16).reshape(capacity, -1)
        d_probs = jnp.einsum(
            "qhd,khd->hqk", d_mixed, value_rows, preferred_element_type=jnp.float32
        )
        d_scores = attn_probs * (d_probs - jnp.sum(d_probs * attn_probs, -1, keepdims=True))
        d_scores = d_scores.astype(jnp.bfloat16)
        d_queries = (
            jnp.einsum("hqk,khd->qhd", d_scores, key_rows, preferred_element_type=jnp.float32)
            * score_scale
        )
        d_queries = d_queries.astype(jnp.bfloat16).reshape(capacity, -1)
        d_keys = (
            jnp.einsum("hqk,qhd->khd", d_scores, queries, preferred_element_type=jnp.float32)
            * score_scale
        )
        d_keys = d_keys.astype(jnp.bfloat16).reshape(capacity, -1)
        g_query = g_query + dense(normed.T, d_queries)
        g_key = g_key + dense(normed.T, d_keys)
        g_value = g_value + dense(normed.T, d_values)
        partial_normed = (
            dense(d_queries, full_query.T)
            + dense(d_keys, full_key.T)
            + dense(d_values, full_value.T)
        )
        d_hidden_half = lax.dynamic_slice_in_dim(d_hidden, offset, half_width, 1)
        route_half = lax.dynamic_slice_in_dim(route_f32, offset, half_width, 0)
        d_normed = lax.psum(partial_normed.astype(jnp.bfloat16), "tensor").astype(jnp.float32)
        norm1_value, norm1_back = jax.vjp(rms_norm, rows_f32, gain1_f32)
        d_rows_norm, d_gain1 = norm1_back(d_normed)
        g_gain1 = g_gain1 + d_gain1
        d_norm_half = lax.dynamic_slice_in_dim(d_rows_norm, offset, half_width, 1)
        g_route = g_route + jnp.dot(
            rows_f32.T, d_logit, precision=lax.Precision.HIGHEST, preferred_element_type=jnp.float32
        )
        d_half = d_hidden_half + d_norm_half + d_logit[:, None] * route_half[None, :]
        grad_rows_new = (cot_half_f32 + d_half).astype(jnp.bfloat16)
        grad_seq = cot_seq.at[chosen].set(grad_rows_new)
        new_gradients = (g_query, g_key, g_value, g_up, g_route, g_gain1, g_gain2, g_out, g_down)
        return (new_gradients, out_seq, grad_seq)

    def micro_step(gradients, micro_inputs):
        tok_micro, routed_micro, cot_micro = micro_inputs
        weight_rows = (
            lax.all_gather(w_query, "dp", axis=0, tiled=True),
            lax.all_gather(w_key, "dp", axis=0, tiled=True),
            lax.all_gather(w_value, "dp", axis=0, tiled=True),
            lax.all_gather(w_up, "dp", axis=0, tiled=True),
            lax.all_gather(w_route, "dp", axis=0, tiled=True),
            lax.all_gather(gain_attn, "dp", axis=0, tiled=True),
            lax.all_gather(gain_mlp, "dp", axis=0, tiled=True),
        )
        weight_cols = (
            lax.all_gather(w_out, "dp", axis=1, tiled=True),
            lax.all_gather(w_down, "dp", axis=1, tiled=True),
        )

        def sequence_scan(carried, seq_inputs):
            tok_seq, chosen, cot_seq = seq_inputs
            updated, out_seq, grad_seq = sequence_step(
                carried, weight_rows, weight_cols, tok_seq, chosen, cot_seq
            )
            return (updated, (out_seq, grad_seq))

        gradients, seq_results = lax.scan(
            sequence_scan, gradients, (tok_micro, routed_micro, cot_micro)
        )
        return (gradients, seq_results)

    zero_grads = (
        jnp.zeros((width, w_query.shape[1]), jnp.float32),
        jnp.zeros((width, w_key.shape[1]), jnp.float32),
        jnp.zeros((width, w_value.shape[1]), jnp.float32),
        jnp.zeros((width, w_up.shape[1]), jnp.float32),
        jnp.zeros((width,), jnp.float32),
        jnp.zeros((width,), jnp.float32),
        jnp.zeros((width,), jnp.float32),
        jnp.zeros((w_out.shape[0], width), jnp.float32),
        jnp.zeros((w_down.shape[0], width), jnp.float32),
    )
    totals, results = lax.scan(micro_step, zero_grads, (tokens, routed, cotangent))
    output, input_grad = results
    g_query, g_key, g_value, g_up, g_route, g_gain1, g_gain2, g_out, g_down = totals
    grad_query, grad_key, grad_value, grad_up, grad_route, grad_gain_attn, grad_gain_mlp = (
        lax.psum_scatter(g_query, "dp", scatter_dimension=0, tiled=True),
        lax.psum_scatter(g_key, "dp", scatter_dimension=0, tiled=True),
        lax.psum_scatter(g_value, "dp", scatter_dimension=0, tiled=True),
        lax.psum_scatter(g_up, "dp", scatter_dimension=0, tiled=True),
        lax.psum_scatter(g_route, "dp", scatter_dimension=0, tiled=True),
        lax.psum_scatter(g_gain1, "dp", scatter_dimension=0, tiled=True),
        lax.psum_scatter(g_gain2, "dp", scatter_dimension=0, tiled=True),
    )
    grad_out, grad_down = (
        lax.psum_scatter(g_out, "dp", scatter_dimension=1, tiled=True),
        lax.psum_scatter(g_down, "dp", scatter_dimension=1, tiled=True),
    )
    return (
        output,
        input_grad,
        grad_query,
        grad_key,
        grad_value,
        grad_out,
        grad_up,
        grad_down,
        grad_route,
        grad_gain_attn,
        grad_gain_mlp,
    )


def solution(mesh):
    placed = (
        P(None, "dp", None, "tensor"),
        P(None, "dp", None),
        P("dp", "tensor"),
        P("dp", "tensor"),
        P("dp", "tensor"),
        P("tensor", "dp"),
        P("dp", "tensor"),
        P("tensor", "dp"),
        P("dp"),
        P("dp"),
        P("dp"),
        P(None, "dp", None, "tensor"),
    )
    return jax.shard_map(
        shards,
        mesh=mesh,
        in_specs=placed,
        out_specs=(
            P(None, "dp", None, "tensor"),
            P(None, "dp", None, "tensor"),
            P("dp", "tensor"),
            P("dp", "tensor"),
            P("dp", "tensor"),
            P("tensor", "dp"),
            P("dp", "tensor"),
            P("tensor", "dp"),
            P("dp"),
            P("dp"),
            P("dp"),
        ),
        check_vma=False,
    )
```

profile of v0, /device:TPU:10, one launch (start us, length us, event | category | flops | bytes accessed | tf_op | source)
XLA Modules:
  0.0 2646.1 jit_solution(17404735948335513344)
XLA Ops:
  8.1 1940.2 %while.33 = (s32[]{:T(128)}, f32[1024,512]{1,0:T(8,128)}, f32[1024,512]{1,0:T(8,128)}, f32[1024,512]{1,0:T(8,128)}, f32[1024,2048]{1,0:T(8,128)}, /*index=5*/f32...) while((s32[]{:T(128)}, f32[1024,512]{1,0:T(8,128)}, ...), condition=%wide.region_17.19_spmd.clone, body=%wide.region_0.18_spmd.clone.sunk | while | flops 11211988992 | bytes 388675808 | solution.py:199
  69.3 55.2 %all-gather.7.cloned.1.call-done = bf16[1024,512]{1,0:T(8,128)(2,1)} async-done(((bf16[64,512]{1,0:T(8,128)(2,1)}), bf16[1024,512]{1,0:T(8,128)(2,1)}) %all-gather.7.cloned.1.call-update) | async-done | bytes 1048592 | tf_op jit(solution)/shard_map/while/body/eval_jaxpr/all_gather | solution.py:164
  126.3 55.0 %all-gather.11.cloned.1.call-done = bf16[1024,512]{1,0:T(8,128)(2,1)} async-done(((bf16[64,512]{1,0:T(8,128)(2,1)}), bf16[1024,512]{1,0:T(8,128)(2,1)}) %all-gather.11.cloned.1.call-update) | async-done | bytes 1048592 | tf_op jit(solution)/shard_map/while/body/eval_jaxpr/all_gather | solution.py:165
  263.0 76.7 %all-gather.15.cloned.1.call-done = bf16[1024,2048]{1,0:T(8,128)(2,1)} async-done(((bf16[64,2048]{1,0:T(8,128)(2,1)}), bf16[1024,2048]{1,0:T(8,128)(2,1)}) %all-gather.15.cloned.1.call-update) | async-done | bytes 4194320 | tf_op jit(solution)/shard_map/while/body/eval_jaxpr/all_gather | solution.py:166
  344.5 73.0 %all-gather.17.cloned.1.call-done = bf16[2048,1024]{0,1:T(8,128)(2,1)} async-done(((bf16[2048,64]{0,1:T(8,128)(2,1)}), bf16[2048,1024]{0,1:T(8,128)(2,1)}) %all-gather.17.cloned.1.call-update) | async-done | bytes 4194320 | tf_op jit(solution)/shard_map/while/body/eval_jaxpr/all_gather | solution.py:173
  554.0 55.2 %all-gather.7.cloned.1.call-done = bf16[1024,512]{1,0:T(8,128)(2,1)} async-done(((bf16[64,512]{1,0:T(8,128)(2,1)}), bf16[1024,512]{1,0:T(8,128)(2,1)}) %all-gather.7.cloned.1.call-update) | async-done | bytes 1048592 | tf_op jit(solution)/shard_map/while/body/eval_jaxpr/all_gather | solution.py:164
  611.0 54.9 %all-gather.11.cloned.1.call-done = bf16[1024,512]{1,0:T(8,128)(2,1)} async-done(((bf16[64,512]{1,0:T(8,128)(2,1)}), bf16[1024,512]{1,0:T(8,128)(2,1)}) %all-gather.11.cloned.1.call-update) | async-done | bytes 1048592 | tf_op jit(solution)/shard_map/while/body/eval_jaxpr/all_gather | solution.py:165
  747.7 76.7 %all-gather.15.cloned.1.call-done = bf16[1024,2048]{1,0:T(8,128)(2,1)} async-done(((bf16[64,2048]{1,0:T(8,128)(2,1)}), bf16[1024,2048]{1,0:T(8,128)(2,1)}) %all-gather.15.cloned.1.call-update) | async-done | bytes 4194320 | tf_op jit(solution)/shard_map/while/body/eval_jaxpr/all_gather | solution.py:166
  829.2 72.8 %all-gather.17.cloned.1.call-done = bf16[2048,1024]{0,1:T(8,128)(2,1)} async-done(((bf16[2048,64]{0,1:T(8,128)(2,1)}), bf16[2048,1024]{0,1:T(8,128)(2,1)}) %all-gather.17.cloned.1.call-update) | async-done | bytes 4194320 | tf_op jit(solution)/shard_map/while/body/eval_jaxpr/all_gather | solution.py:173
  1038.9 55.0 %all-gather.7.cloned.1.call-done = bf16[1024,512]{1,0:T(8,128)(2,1)} async-done(((bf16[64,512]{1,0:T(8,128)(2,1)}), bf16[1024,512]{1,0:T(8,128)(2,1)}) %all-gather.7.cloned.1.call-update) | async-done | bytes 1048592 | tf_op jit(solution)/shard_map/while/body/eval_jaxpr/all_gather | solution.py:164
  1095.7 55.0 %all-gather.11.cloned.1.call-done = bf16[1024,512]{1,0:T(8,128)(2,1)} async-done(((bf16[64,512]{1,0:T(8,128)(2,1)}), bf16[1024,512]{1,0:T(8,128)(2,1)}) %all-gather.11.cloned.1.call-update) | async-done | bytes 1048592 | tf_op jit(solution)/shard_map/while/body/eval_jaxpr/all_gather | solution.py:165
  1232.7 76.7 %all-gather.15.cloned.1.call-done = bf16[1024,2048]{1,0:T(8,128)(2,1)} async-done(((bf16[64,2048]{1,0:T(8,128)(2,1)}), bf16[1024,2048]{1,0:T(8,128)(2,1)}) %all-gather.15.cloned.1.call-update) | async-done | bytes 4194320 | tf_op jit(solution)/shard_map/while/body/eval_jaxpr/all_gather | solution.py:166
  1314.2 73.0 %all-gather.17.cloned.1.call-done = bf16[2048,1024]{0,1:T(8,128)(2,1)} async-done(((bf16[2048,64]{0,1:T(8,128)(2,1)}), bf16[2048,1024]{0,1:T(8,128)(2,1)}) %all-gather.17.cloned.1.call-update) | async-done | bytes 4194320 | tf_op jit(solution)/shard_map/while/body/eval_jaxpr/all_gather | solution.py:173
  1524.0 55.2 %all-gather.7.cloned.1.call-done = bf16[1024,512]{1,0:T(8,128)(2,1)} async-done(((bf16[64,512]{1,0:T(8,128)(2,1)}), bf16[1024,512]{1,0:T(8,128)(2,1)}) %all-gather.7.cloned.1.call-update) | async-done | bytes 1048592 | tf_op jit(solution)/shard_map/while/body/eval_jaxpr/all_gather | solution.py:164
  1581.0 54.9 %all-gather.11.cloned.1.call-done = bf16[1024,512]{1,0:T(8,128)(2,1)} async-done(((bf16[64,512]{1,0:T(8,128)(2,1)}), bf16[1024,512]{1,0:T(8,128)(2,1)}) %all-gather.11.cloned.1.call-update) | async-done | bytes 1048592 | tf_op jit(solution)/shard_map/while/body/eval_jaxpr/all_gather | solution.py:165
  1639.1 53.7 %all-gather.13.cloned.1.call-done = bf16[512,1024]{0,1:T(8,128)(2,1)} async-done(((bf16[512,64]{0,1:T(8,128)(2,1)}), bf16[512,1024]{0,1:T(8,128)(2,1)}) %all-gather.13.cloned.1.call-update) | async-done | bytes 1048592 | tf_op jit(solution)/shard_map/while/body/eval_jaxpr/all_gather | solution.py:172
  1717.9 76.7 %all-gather.15.cloned.1.call-done = bf16[1024,2048]{1,0:T(8,128)(2,1)} async-done(((bf16[64,2048]{1,0:T(8,128)(2,1)}), bf16[1024,2048]{1,0:T(8,128)(2,1)}) %all-gather.15.cloned.1.call-update) | async-done | bytes 4194320 | tf_op jit(solution)/shard_map/while/body/eval_jaxpr/all_gather | solution.py:166
  1799.4 73.0 %all-gather.17.cloned.1.call-done = bf16[2048,1024]{0,1:T(8,128)(2,1)} async-done(((bf16[2048,64]{0,1:T(8,128)(2,1)}), bf16[2048,1024]{0,1:T(8,128)(2,1)}) %all-gather.17.cloned.1.call-update) | async-done | bytes 4194320 | tf_op jit(solution)/shard_map/while/body/eval_jaxpr/all_gather | solution.py:173
  1964.4 65.4 %all-reduce.11 = (f32[1024]{0:T(1024)S(1)}, f32[1024]{0:T(1024)S(1)}, f32[1024]{0:T(1024)S(1)}) all-reduce(f32[1024]{0:T(1024)S(1)} %get-tuple-element.429, f32[1024]{0:T(1024)S(1)} %get-tuple-element.430, f32[1024]{0:T(1024)S(1)} %get-tuple-element.431), channel_id=8, replica_groups=mesh['dp'=16,'tensor'=2] {'dp'}, use_global_device_ids=true, to_apply=%region_24.26.clone | all-reduce | flops 3072 | bytes 24576
  2031.5 72.3 %reduce-scatter.11.cloned.1.call-done = f32[64,512]{1,0:T(8,128)} async-done(((f32[1024,512]{1,0:T(8,128)}), f32[64,512]{1,0:T(8,128)}) %reduce-scatter.11.cloned.1.call-update) | async-done | bytes 131088 | tf_op jit(solution)/shard_map/reduce_scatter | solution.py:205
  2103.9 80.7 %reduce-scatter.7.cloned.1.call-done = f32[64,512]{1,0:T(8,128)} async-done(((f32[1024,512]{1,0:T(8,128)}), f32[64,512]{1,0:T(8,128)}) %reduce-scatter.7.cloned.1.call-update) | async-done | bytes 131088 | tf_op jit(solution)/shard_map/reduce_scatter | solution.py:203
  2184.6 80.9 %reduce-scatter.9.cloned.1.call-done = f32[64,512]{1,0:T(8,128)} async-done(((f32[1024,512]{1,0:T(8,128)}), f32[64,512]{1,0:T(8,128)}) %reduce-scatter.9.cloned.1.call-update) | async-done | bytes 131088 | tf_op jit(solution)/shard_map/reduce_scatter | solution.py:204
  2265.5 190.3 %reduce-scatter.17.cloned.1.call-done = f32[2048,64]{0,1:T(8,128)} async-done(((f32[2048,1024]{0,1:T(8,128)}), f32[2048,64]{0,1:T(8,128)}) %reduce-scatter.17.cloned.1.call-update) | async-done | bytes 524304 | tf_op jit(solution)/shard_map/reduce_scatter | solution.py:213
  2455.9 183.1 %reduce-scatter.15.cloned.1.call-done = f32[64,2048]{1,0:T(8,128)} async-done(((f32[1024,2048]{1,0:T(8,128)}), f32[64,2048]{1,0:T(8,128)}) %reduce-scatter.15.cloned.1.call-update) | async-done | bytes 524304 | tf_op jit(solution)/shard_map/reduce_scatter | solution.py:206
  (759 shorter events, 859.2 us)
Async XLA Ops:
  9.6 171.7 %all-gather.11.cloned.1.call-start = ((), (), s32[]{:S(2)}) async-start(), calls=%async_computation.14 | async-start | bytes 1114112 | tf_op jit(solution)/shard_map/while/body/eval_jaxpr/all_gather | solution.py:165
  10.4 227.7 %all-gather.13.cloned.1.call-start = ((), (), s32[]{:S(2)}) async-start(), calls=%async_computation.15 | async-start | bytes 1114112 | tf_op jit(solution)/shard_map/while/body/eval_jaxpr/all_gather | solution.py:172
  10.9 248.7 %all-reduce.20.cloned.1.call-start = ((), (), s32[]{:S(2)}) async-start(), calls=%async_computation.16 | async-start | bytes 1048576 | tf_op jit(solution)/shard_map/while/body/eval_jaxpr/while/body/eval_jaxpr/psum | solution.py:74
  241.2 176.3 %all-gather.17.cloned.1.call-start = ((), (), s32[]{:S(2)}) async-start(), calls=%async_computation.18 | async-start | bytes 4456448 | tf_op jit(solution)/shard_map/while/body/eval_jaxpr/all_gather | solution.py:173
  241.9 209.8 %all-reduce.22.cloned.1.call-start = ((), (), s32[]{:S(2)}) async-start(), calls=%async_computation.19 | async-start | bytes 2097152 | tf_op jit(solution)/shard_map/while/body/eval_jaxpr/while/body/eval_jaxpr/psum | solution.py:101
  494.7 171.2 %all-gather.11.cloned.1.call-start = ((), (), s32[]{:S(2)}) async-start(), calls=%async_computation.14 | async-start | bytes 1114112 | tf_op jit(solution)/shard_map/while/body/eval_jaxpr/all_gather | solution.py:165
  495.3 227.5 %all-gather.13.cloned.1.call-start = ((), (), s32[]{:S(2)}) async-start(), calls=%async_computation.15 | async-start | bytes 1114112 | tf_op jit(solution)/shard_map/while/body/eval_jaxpr/all_gather | solution.py:172
  496.1 248.3 %all-reduce.20.cloned.1.call-start = ((), (), s32[]{:S(2)}) async-start(), calls=%async_computation.16 | async-start | bytes 1048576 | tf_op jit(solution)/shard_map/while/body/eval_jaxpr/while/body/eval_jaxpr/psum | solution.py:74
  725.9 176.2 %all-gather.17.cloned.1.call-start = ((), (), s32[]{:S(2)}) async-start(), calls=%async_computation.18 | async-start | bytes 4456448 | tf_op jit(solution)/shard_map/while/body/eval_jaxpr/all_gather | solution.py:173
  726.5 209.8 %all-reduce.22.cloned.1.call-start = ((), (), s32[]{:S(2)}) async-start(), calls=%async_computation.19 | async-start | bytes 2097152 | tf_op jit(solution)/shard_map/while/body/eval_jaxpr/while/body/eval_jaxpr/psum | solution.py:101
  979.3 171.5 %all-gather.11.cloned.1.call-start = ((), (), s32[]{:S(2)}) async-start(), calls=%async_computation.14 | async-start | bytes 1114112 | tf_op jit(solution)/shard_map/while/body/eval_jaxpr/all_gather | solution.py:165
  980.0 227.6 %all-gather.13.cloned.1.call-start = ((), (), s32[]{:S(2)}) async-start(), calls=%async_computation.15 | async-start | bytes 1114112 | tf_op jit(solution)/shard_map/while/body/eval_jaxpr/all_gather | solution.py:172
  980.8 248.6 %all-reduce.20.cloned.1.call-start = ((), (), s32[]{:S(2)}) async-start(), calls=%async_computation.16 | async-start | bytes 1048576 | tf_op jit(solution)/shard_map/while/body/eval_jaxpr/while/body/eval_jaxpr/psum | solution.py:74
  1210.7 176.5 %all-gather.17.cloned.1.call-start = ((), (), s32[]{:S(2)}) async-start(), calls=%async_computation.18 | async-start | bytes 4456448 | tf_op jit(solution)/shard_map/while/body/eval_jaxpr/all_gather | solution.py:173
  1211.5 209.9 %all-reduce.22.cloned.1.call-start = ((), (), s32[]{:S(2)}) async-start(), calls=%async_computation.19 | async-start | bytes 2097152 | tf_op jit(solution)/shard_map/while/body/eval_jaxpr/while/body/eval_jaxpr/psum | solution.py:101
  1464.6 171.3 %all-gather.11.cloned.1.call-start = ((), (), s32[]{:S(2)}) async-start(), calls=%async_computation.14 | async-start | bytes 1114112 | tf_op jit(solution)/shard_map/while/body/eval_jaxpr/all_gather | solution.py:165
  1465.2 227.6 %all-gather.13.cloned.1.call-start = ((), (), s32[]{:S(2)}) async-start(), calls=%async_computation.15 | async-start | bytes 1114112 | tf_op jit(solution)/shard_map/while/body/eval_jaxpr/all_gather | solution.py:172
  1465.9 248.6 %all-reduce.20.cloned.1.call-start = ((), (), s32[]{:S(2)}) async-start(), calls=%async_computation.16 | async-start | bytes 1048576 | tf_op jit(solution)/shard_map/while/body/eval_jaxpr/while/body/eval_jaxpr/psum | solution.py:74
  1695.9 176.5 %all-gather.17.cloned.1.call-start = ((), (), s32[]{:S(2)}) async-start(), calls=%async_computation.18 | async-start | bytes 4456448 | tf_op jit(solution)/shard_map/while/body/eval_jaxpr/all_gather | solution.py:173
  1696.6 209.9 %all-reduce.22.cloned.1.call-start = ((), (), s32[]{:S(2)}) async-start(), calls=%async_computation.19 | async-start | bytes 2097152 | tf_op jit(solution)/shard_map/while/body/eval_jaxpr/while/body/eval_jaxpr/psum | solution.py:101
  1951.8 232.8 %reduce-scatter.7.cloned.1.call-start = ((), (), s32[]{:S(2)}) async-start(), calls=%async_computation.6 | async-start | bytes 2228224 | tf_op jit(solution)/shard_map/reduce_scatter | solution.py:203
  1952.4 313.1 %reduce-scatter.9.cloned.1.call-start = ((), (), s32[]{:S(2)}) async-start(), calls=%async_computation.7 | async-start | bytes 2228224 | tf_op jit(solution)/shard_map/reduce_scatter | solution.py:204
  1953.1 502.7 %reduce-scatter.17.cloned.1.call-start = ((), (), s32[]{:S(2)}) async-start(), calls=%async_computation.11 | async-start | bytes 8912896 | tf_op jit(solution)/shard_map/reduce_scatter | solution.py:213
  1962.4 676.5 %reduce-scatter.15.cloned.1.call-start = ((), (), s32[]{:S(2)}) async-start(), calls=%async_computation.10 | async-start | bytes 8912896 | tf_op jit(solution)/shard_map/reduce_scatter | solution.py:206
  (183 other events, 2725.6 us)
Sparse Core Ops, SparseCore 0:
  11.7 55.6 all-gather.8
  70.2 54.2 all-gather.6
  127.2 54.0 all-gather.10
  184.0 54.0 all-gather.12
  262.6 76.9 all-gather.14
  342.8 74.6 all-gather.16
  496.7 55.4 all-gather.8
  554.9 54.2 all-gather.6
  611.8 54.0 all-gather.10
  668.7 54.0 all-gather.12
  747.3 76.9 all-gather.14
  827.3 74.6 all-gather.16
  981.6 55.4 all-gather.8
  1039.6 54.2 all-gather.6
  1096.6 54.0 all-gather.10
  1153.5 54.0 all-gather.12
  1232.3 76.9 all-gather.14
  1312.5 74.6 all-gather.16
  1466.7 55.4 all-gather.8
  1524.9 54.2 all-gather.6
  1581.8 54.0 all-gather.10
  1638.7 54.0 all-gather.12
  1717.5 76.9 all-gather.14
  1797.7 74.6 all-gather.16
  (12 shorter events, 228.2 us)
Sparse Core Ops, SparseCore 1:
  1951.6 72.0 reduce-scatter.12
  2026.4 77.5 reduce-scatter.10
  2106.6 77.9 reduce-scatter.6
  2187.5 78.0 reduce-scatter.8
  2268.4 187.4 reduce-scatter.16
  2458.7 180.1 reduce-scatter.14
where the time goes:
time: 2650 us
  waiting for transfers between devices  2020 us (76%)
  matrix products  212 us (8%)
  blocking collectives  209 us (8%)
  local copies, waits for them, and re-layouts  103 us (4%)
  other arithmetic  83.7 us (3%)
    all_gather x4, waiting for transfers between devices, micro_step(): lax.all_gather(w_up, 'dp', axis=0, tiled=True)  307 us
    all_gather x4, waiting for transfers between devices, micro_step(): lax.all_gather(w_down, 'dp', axis=1, tiled=True)  292 us
    all_gather x4, waiting for transfers between devices, micro_step(): lax.all_gather(w_key, 'dp', axis=0, tiled=True)  221 us
    all_gather x4, waiting for transfers between devices, micro_step(): lax.all_gather(w_value, 'dp', axis=0, tiled=True)  220 us
    all_gather x4, waiting for transfers between devices, micro_step(): lax.all_gather(w_out, 'dp', axis=1, tiled=True)  215 us
    dot_general x76, matrix products, dense(): return jnp.dot(left, right, preferred_element_type=jnp.float32)  200 us
    reduce_scatter x1, waiting for transfers between devices, shards(): lax.psum_scatter(g_down, 'dp', scatter_dimension=1, tiled=True)  190 us
    reduce_scatter x1, waiting for transfers between devices, shards(): lax.psum_scatter(g_up, 'dp', scatter_dimension=0, tiled=True)  183 us
  transfers between devices with their start and end apart: 42, of which 41 were waited for; matrix products, arithmetic and copies ran while one was open for 8% of the time, Pallas kernels for 0%

commit v1 on v0

--- a/solution.py
+++ b/solution.py
@@ -5,6 +5,28 @@
 
 HD = 64
 eps_norm = 1e-05
+
+
+def laid_out(blocks, dim):
+    blocks = jnp.moveaxis(blocks, 0, dim)
+    shape = blocks.shape
+    return blocks.reshape(*shape[:dim], shape[dim] * shape[dim + 1], *shape[dim + 2 :])
+
+
+def gather_around(shard, axis, dim):
+    length = lax.axis_size(axis)
+    pairs = [(i, (i + 1) % length) for i in range(length)]
+    back = [(b, a) for a, b in pairs]
+    lower, upper = ([], [])
+    for step in range(length - 1):
+        if step % 2 == 0:
+            lower.append(lax.ppermute(lower[-1] if lower else shard, axis, pairs))
+        else:
+            upper.append(lax.ppermute(upper[-1] if upper else shard, axis, back))
+    tiles = jnp.stack([*lower[::-1], shard, *upper])
+    shift = lax.axis_index(axis) - len(lower)
+    tiles = tiles[(jnp.arange(length) - shift) % length]
+    return laid_out(tiles, dim)
 
 
 def rms_norm(values, gain):
@@ -169,7 +191,7 @@
             lax.all_gather(gain_mlp, "dp", axis=0, tiled=True),
         )
         weight_cols = (
-            lax.all_gather(w_out, "dp", axis=1, tiled=True),
+            gather_around(w_out, "dp", 1),
             lax.all_gather(w_down, "dp", axis=1, tiled=True),
         )
 

time: 2650 us -> 2490 us (0.940)
  waiting for transfers between devices: 2020 us -> 1820 us
    all_gather x4 -> x0, waiting for transfers between devices: 215 us -> none  [micro_step(): lax.all_gather(w_out, 'dp', axis=1, tiled=True)]
  transfers between devices with their start and end apart: 42 -> 53, of which waited for: 41 -> 51; matrix products, arithmetic and copies ran while one was open for 8% -> 9% of each run, Pallas kernels for 0% -> 0%
where the time goes in v1:
time: 2490 us
  waiting for transfers between devices  1820 us (73%)
  blocking collectives  227 us (9%)
  matrix products  207 us (8%)
  local copies, waits for them, and re-layouts  108 us (4%)
  other arithmetic  84.1 us (3%)
    all_gather x4, waiting for transfers between devices, micro_step(): lax.all_gather(w_up, 'dp', axis=0, tiled=True)  307 us
    all_gather x4, waiting for transfers between devices, micro_step(): lax.all_gather(w_down, 'dp', axis=1, tiled=True)  291 us
    all_gather x4, waiting for transfers between devices, micro_step(): lax.all_gather(w_key, 'dp', axis=0, tiled=True)  221 us
    all_gather x4, waiting for transfers between devices, micro_step(): lax.all_gather(w_value, 'dp', axis=0, tiled=True)  216 us
    dot_general x76, matrix products, dense(): return jnp.dot(left, right, preferred_element_type=jnp.float32)  195 us
    reduce_scatter x1, waiting for transfers between devices, shards(): lax.psum_scatter(g_down, 'dp', scatter_dimension=1, tiled=True)  190 us
    reduce_scatter x1, waiting for transfers between devices, shards(): lax.psum_scatter(g_up, 'dp', scatter_dimension=0, tiled=True)  183 us
    while x4, blocking collectives  143 us
  transfers between devices with their start and end apart: 53, of which 51 were waited for; matrix products, arithmetic and copies ran while one was open for 9% of the time, Pallas kernels for 0%

profile of v1, /device:TPU:10, one launch (start us, length us, event | category | flops | bytes accessed | tf_op | source)
XLA Modules:
  0.0 2491.0 jit_solution(150506512897950998)
XLA Ops:
  57.0 1736.9 %while.35 = (s32[]{:T(128)}, f32[1024,512]{1,0:T(8,128)}, f32[1024,512]{1,0:T(8,128)}, f32[1024,512]{1,0:T(8,128)}, f32[1024,2048]{1,0:T(8,128)}, /*index=5*/f32...) while((s32[]{:T(128)}, f32[1024,512]{1,0:T(8,128)}, ...), condition=%wide.region_17.19_spmd.clone, body=%wide.region_0.18_spmd.clone.sunk | while | flops 11211988992 | bytes 389525600 | solution.py:221
  73.7 48.9 %all-reduce.14 = (bf16[1024]{0:T(1024)(128)(2,1)S(1)}, bf16[1024]{0:T(1024)(128)(2,1)S(1)}, bf16[1024]{0:T(1024)(128)(2,1)S(1)}) all-reduce(bf16[1024]{0:T(1024)(128)(2,1)S(1)} %dynamic-update-slice.41, bf16[1024]{0:T(1024)(128)(2,1)S(1)} %dynamic-update-slice.42, ...), channel_id=1, replica_groups=mesh['dp'=16,'tensor'=2] {'dp'}, use_global_device_ids=true, to_apply=%add.1 | all-reduce | flops 3072 | bytes 12288 | tf_op jit(solution)/shard_map/while
  134.9 55.2 %all-gather.6.cloned.1.call-done = bf16[1024,512]{1,0:T(8,128)(2,1)} async-done(((bf16[64,512]{1,0:T(8,128)(2,1)}), bf16[1024,512]{1,0:T(8,128)(2,1)}) %all-gather.6.cloned.1.call-update) | async-done | bytes 1048592 | tf_op jit(solution)/shard_map/while/body/eval_jaxpr/all_gather | solution.py:186
  192.9 54.1 %all-gather.10.cloned.1.call-done = bf16[1024,512]{1,0:T(8,128)(2,1)} async-done(((bf16[64,512]{1,0:T(8,128)(2,1)}), bf16[1024,512]{1,0:T(8,128)(2,1)}) %all-gather.10.cloned.1.call-update) | async-done | bytes 1048592 | tf_op jit(solution)/shard_map/while/body/eval_jaxpr/all_gather | solution.py:187
  273.8 76.7 %all-gather.12.cloned.1.call-done = bf16[1024,2048]{1,0:T(8,128)(2,1)} async-done(((bf16[64,2048]{1,0:T(8,128)(2,1)}), bf16[1024,2048]{1,0:T(8,128)(2,1)}) %all-gather.12.cloned.1.call-update) | async-done | bytes 4194320 | tf_op jit(solution)/shard_map/while/body/eval_jaxpr/all_gather | solution.py:188
  355.4 72.8 %all-gather.14.cloned.1.call-done = bf16[2048,1024]{0,1:T(8,128)(2,1)} async-done(((bf16[2048,64]{0,1:T(8,128)(2,1)}), bf16[2048,1024]{0,1:T(8,128)(2,1)}) %all-gather.14.cloned.1.call-update) | async-done | bytes 4194320 | tf_op jit(solution)/shard_map/while/body/eval_jaxpr/all_gather | solution.py:195
  565.0 55.1 %all-gather.6.cloned.1.call-done = bf16[1024,512]{1,0:T(8,128)(2,1)} async-done(((bf16[64,512]{1,0:T(8,128)(2,1)}), bf16[1024,512]{1,0:T(8,128)(2,1)}) %all-gather.6.cloned.1.call-update) | async-done | bytes 1048592 | tf_op jit(solution)/shard_map/while/body/eval_jaxpr/all_gather | solution.py:186
  622.8 54.1 %all-gather.10.cloned.1.call-done = bf16[1024,512]{1,0:T(8,128)(2,1)} async-done(((bf16[64,512]{1,0:T(8,128)(2,1)}), bf16[1024,512]{1,0:T(8,128)(2,1)}) %all-gather.10.cloned.1.call-update) | async-done | bytes 1048592 | tf_op jit(solution)/shard_map/while/body/eval_jaxpr/all_gather | solution.py:187
  703.7 76.8 %all-gather.12.cloned.1.call-done = bf16[1024,2048]{1,0:T(8,128)(2,1)} async-done(((bf16[64,2048]{1,0:T(8,128)(2,1)}), bf16[1024,2048]{1,0:T(8,128)(2,1)}) %all-gather.12.cloned.1.call-update) | async-done | bytes 4194320 | tf_op jit(solution)/shard_map/while/body/eval_jaxpr/all_gather | solution.py:188
  785.4 72.8 %all-gather.14.cloned.1.call-done = bf16[2048,1024]{0,1:T(8,128)(2,1)} async-done(((bf16[2048,64]{0,1:T(8,128)(2,1)}), bf16[2048,1024]{0,1:T(8,128)(2,1)}) %all-gather.14.cloned.1.call-update) | async-done | bytes 4194320 | tf_op jit(solution)/shard_map/while/body/eval_jaxpr/all_gather | solution.py:195
  994.7 55.1 %all-gather.6.cloned.1.call-done = bf16[1024,512]{1,0:T(8,128)(2,1)} async-done(((bf16[64,512]{1,0:T(8,128)(2,1)}), bf16[1024,512]{1,0:T(8,128)(2,1)}) %all-gather.6.cloned.1.call-update) | async-done | bytes 1048592 | tf_op jit(solution)/shard_map/while/body/eval_jaxpr/all_gather | solution.py:186
  1052.5 54.1 %all-gather.10.cloned.1.call-done = bf16[1024,512]{1,0:T(8,128)(2,1)} async-done(((bf16[64,512]{1,0:T(8,128)(2,1)}), bf16[1024,512]{1,0:T(8,128)(2,1)}) %all-gather.10.cloned.1.call-update) | async-done | bytes 1048592 | tf_op jit(solution)/shard_map/while/body/eval_jaxpr/all_gather | solution.py:187
  1133.4 76.8 %all-gather.12.cloned.1.call-done = bf16[1024,2048]{1,0:T(8,128)(2,1)} async-done(((bf16[64,2048]{1,0:T(8,128)(2,1)}), bf16[1024,2048]{1,0:T(8,128)(2,1)}) %all-gather.12.cloned.1.call-update) | async-done | bytes 4194320 | tf_op jit(solution)/shard_map/while/body/eval_jaxpr/all_gather | solution.py:188
  1215.2 72.9 %all-gather.14.cloned.1.call-done = bf16[2048,1024]{0,1:T(8,128)(2,1)} async-done(((bf16[2048,64]{0,1:T(8,128)(2,1)}), bf16[2048,1024]{0,1:T(8,128)(2,1)}) %all-gather.14.cloned.1.call-update) | async-done | bytes 4194320 | tf_op jit(solution)/shard_map/while/body/eval_jaxpr/all_gather | solution.py:195
  1424.8 55.1 %all-gather.6.cloned.1.call-done = bf16[1024,512]{1,0:T(8,128)(2,1)} async-done(((bf16[64,512]{1,0:T(8,128)(2,1)}), bf16[1024,512]{1,0:T(8,128)(2,1)}) %all-gather.6.cloned.1.call-update) | async-done | bytes 1048592 | tf_op jit(solution)/shard_map/while/body/eval_jaxpr/all_gather | solution.py:186
  1482.7 54.0 %all-gather.10.cloned.1.call-done = bf16[1024,512]{1,0:T(8,128)(2,1)} async-done(((bf16[64,512]{1,0:T(8,128)(2,1)}), bf16[1024,512]{1,0:T(8,128)(2,1)}) %all-gather.10.cloned.1.call-update) | async-done | bytes 1048592 | tf_op jit(solution)/shard_map/while/body/eval_jaxpr/all_gather | solution.py:187
  1563.4 76.8 %all-gather.12.cloned.1.call-done = bf16[1024,2048]{1,0:T(8,128)(2,1)} async-done(((bf16[64,2048]{1,0:T(8,128)(2,1)}), bf16[1024,2048]{1,0:T(8,128)(2,1)}) %all-gather.12.cloned.1.call-update) | async-done | bytes 4194320 | tf_op jit(solution)/shard_map/while/body/eval_jaxpr/all_gather | solution.py:188
  1645.2 72.8 %all-gather.14.cloned.1.call-done = bf16[2048,1024]{0,1:T(8,128)(2,1)} async-done(((bf16[2048,64]{0,1:T(8,128)(2,1)}), bf16[2048,1024]{0,1:T(8,128)(2,1)}) %all-gather.14.cloned.1.call-update) | async-done | bytes 4194320 | tf_op jit(solution)/shard_map/while/body/eval_jaxpr/all_gather | solution.py:195
  1810.0 65.5 %all-reduce.11 = (f32[1024]{0:T(1024)S(1)}, f32[1024]{0:T(1024)S(1)}, f32[1024]{0:T(1024)S(1)}) all-reduce(f32[1024]{0:T(1024)S(1)} %get-tuple-element.609, f32[1024]{0:T(1024)S(1)} %get-tuple-element.610, f32[1024]{0:T(1024)S(1)} %get-tuple-element.611), channel_id=8, replica_groups=mesh['dp'=16,'tensor'=2] {'dp'}, use_global_device_ids=true, to_apply=%region_24.26.clone | all-reduce | flops 3072 | bytes 24576
  1877.3 72.1 %reduce-scatter.11.cloned.1.call-done = f32[64,512]{1,0:T(8,128)} async-done(((f32[1024,512]{1,0:T(8,128)}), f32[64,512]{1,0:T(8,128)}) %reduce-scatter.11.cloned.1.call-update) | async-done | bytes 131088 | tf_op jit(solution)/shard_map/reduce_scatter | solution.py:227
  1949.4 80.6 %reduce-scatter.7.cloned.1.call-done = f32[64,512]{1,0:T(8,128)} async-done(((f32[1024,512]{1,0:T(8,128)}), f32[64,512]{1,0:T(8,128)}) %reduce-scatter.7.cloned.1.call-update) | async-done | bytes 131088 | tf_op jit(solution)/shard_map/reduce_scatter | solution.py:225
  2030.0 80.4 %reduce-scatter.9.cloned.1.call-done = f32[64,512]{1,0:T(8,128)} async-done(((f32[1024,512]{1,0:T(8,128)}), f32[64,512]{1,0:T(8,128)}) %reduce-scatter.9.cloned.1.call-update) | async-done | bytes 131088 | tf_op jit(solution)/shard_map/reduce_scatter | solution.py:226
  2110.4 190.4 %reduce-scatter.17.cloned.1.call-done = f32[2048,64]{0,1:T(8,128)} async-done(((f32[2048,1024]{0,1:T(8,128)}), f32[2048,64]{0,1:T(8,128)}) %reduce-scatter.17.cloned.1.call-update) | async-done | bytes 524304 | tf_op jit(solution)/shard_map/reduce_scatter | solution.py:235
  2300.8 183.1 %reduce-scatter.15.cloned.1.call-done = f32[64,2048]{1,0:T(8,128)} async-done(((f32[1024,2048]{1,0:T(8,128)}), f32[64,2048]{1,0:T(8,128)}) %reduce-scatter.15.cloned.1.call-update) | async-done | bytes 524304 | tf_op jit(solution)/shard_map/reduce_scatter | solution.py:228
  (778 shorter events, 713.1 us)
Async XLA Ops:
  57.7 132.4 %all-gather.6.cloned.1.call-start = ((), (), s32[]{:S(2)}) async-start(), calls=%async_computation.12 | async-start | bytes 1114112 | tf_op jit(solution)/shard_map/while/body/eval_jaxpr/all_gather | solution.py:186
  58.5 188.5 %all-gather.10.cloned.1.call-start = ((), (), s32[]{:S(2)}) async-start(), calls=%async_computation.14 | async-start | bytes 1114112 | tf_op jit(solution)/shard_map/while/body/eval_jaxpr/all_gather | solution.py:187
  59.2 211.2 %all-reduce.20.cloned.1.call-start = ((), (), s32[]{:S(2)}) async-start(), calls=%async_computation.15 | async-start | bytes 1048576 | tf_op jit(solution)/shard_map/while/body/eval_jaxpr/while/body/eval_jaxpr/psum | solution.py:96
  252.1 176.1 %all-gather.14.cloned.1.call-start = ((), (), s32[]{:S(2)}) async-start(), calls=%async_computation.17 | async-start | bytes 4456448 | tf_op jit(solution)/shard_map/while/body/eval_jaxpr/all_gather | solution.py:195
  252.7 209.6 %all-reduce.22.cloned.1.call-start = ((), (), s32[]{:S(2)}) async-start(), calls=%async_computation.18 | async-start | bytes 2097152 | tf_op jit(solution)/shard_map/while/body/eval_jaxpr/while/body/eval_jaxpr/psum | solution.py:123
  504.8 115.3 %all-gather.6.cloned.1.call-start = ((), (), s32[]{:S(2)}) async-start(), calls=%async_computation.12 | async-start | bytes 1114112 | tf_op jit(solution)/shard_map/while/body/eval_jaxpr/all_gather | solution.py:186
  505.4 171.5 %all-gather.10.cloned.1.call-start = ((), (), s32[]{:S(2)}) async-start(), calls=%async_computation.14 | async-start | bytes 1114112 | tf_op jit(solution)/shard_map/while/body/eval_jaxpr/all_gather | solution.py:187
  506.1 194.2 %all-reduce.20.cloned.1.call-start = ((), (), s32[]{:S(2)}) async-start(), calls=%async_computation.15 | async-start | bytes 1048576 | tf_op jit(solution)/shard_map/while/body/eval_jaxpr/while/body/eval_jaxpr/psum | solution.py:96
  682.2 176.0 %all-gather.14.cloned.1.call-start = ((), (), s32[]{:S(2)}) async-start(), calls=%async_computation.17 | async-start | bytes 4456448 | tf_op jit(solution)/shard_map/while/body/eval_jaxpr/all_gather | solution.py:195
  682.7 209.6 %all-reduce.22.cloned.1.call-start = ((), (), s32[]{:S(2)}) async-start(), calls=%async_computation.18 | async-start | bytes 2097152 | tf_op jit(solution)/shard_map/while/body/eval_jaxpr/while/body/eval_jaxpr/psum | solution.py:123
  935.3 171.4 %all-gather.10.cloned.1.call-start = ((), (), s32[]{:S(2)}) async-start(), calls=%async_computation.14 | async-start | bytes 1114112 | tf_op jit(solution)/shard_map/while/body/eval_jaxpr/all_gather | solution.py:187
  936.1 194.0 %all-reduce.20.cloned.1.call-start = ((), (), s32[]{:S(2)}) async-start(), calls=%async_computation.15 | async-start | bytes 1048576 | tf_op jit(solution)/shard_map/while/body/eval_jaxpr/while/body/eval_jaxpr/psum | solution.py:96
  1111.9 176.2 %all-gather.14.cloned.1.call-start = ((), (), s32[]{:S(2)}) async-start(), calls=%async_computation.17 | async-start | bytes 4456448 | tf_op jit(solution)/shard_map/while/body/eval_jaxpr/all_gather | solution.py:195
  1112.6 209.6 %all-reduce.22.cloned.1.call-start = ((), (), s32[]{:S(2)}) async-start(), calls=%async_computation.18 | async-start | bytes 2097152 | tf_op jit(solution)/shard_map/while/body/eval_jaxpr/while/body/eval_jaxpr/psum | solution.py:123
  1364.8 115.2 %all-gather.6.cloned.1.call-start = ((), (), s32[]{:S(2)}) async-start(), calls=%async_computation.12 | async-start | bytes 1114112 | tf_op jit(solution)/shard_map/while/body/eval_jaxpr/all_gather | solution.py:186
  1365.4 171.3 %all-gather.10.cloned.1.call-start = ((), (), s32[]{:S(2)}) async-start(), calls=%async_computation.14 | async-start | bytes 1114112 | tf_op jit(solution)/shard_map/while/body/eval_jaxpr/all_gather | solution.py:187
  1365.9 194.1 %all-reduce.20.cloned.1.call-start = ((), (), s32[]{:S(2)}) async-start(), calls=%async_computation.15 | async-start | bytes 1048576 | tf_op jit(solution)/shard_map/while/body/eval_jaxpr/while/body/eval_jaxpr/psum | solution.py:96
  1541.9 176.1 %all-gather.14.cloned.1.call-start = ((), (), s32[]{:S(2)}) async-start(), calls=%async_computation.17 | async-start | bytes 4456448 | tf_op jit(solution)/shard_map/while/body/eval_jaxpr/all_gather | solution.py:195
  1542.5 209.6 %all-reduce.22.cloned.1.call-start = ((), (), s32[]{:S(2)}) async-start(), calls=%async_computation.18 | async-start | bytes 2097152 | tf_op jit(solution)/shard_map/while/body/eval_jaxpr/while/body/eval_jaxpr/psum | solution.py:123
  1796.8 152.6 %reduce-scatter.11.cloned.1.call-start = ((), (), s32[]{:S(2)}) async-start(), calls=%async_computation.8 | async-start | bytes 2228224 | tf_op jit(solution)/shard_map/reduce_scatter | solution.py:227
  1797.4 232.6 %reduce-scatter.7.cloned.1.call-start = ((), (), s32[]{:S(2)}) async-start(), calls=%async_computation.6 | async-start | bytes 2228224 | tf_op jit(solution)/shard_map/reduce_scatter | solution.py:225
  1798.0 312.4 %reduce-scatter.9.cloned.1.call-start = ((), (), s32[]{:S(2)}) async-start(), calls=%async_computation.7 | async-start | bytes 2228224 | tf_op jit(solution)/shard_map/reduce_scatter | solution.py:226
  1798.7 502.1 %reduce-scatter.17.cloned.1.call-start = ((), (), s32[]{:S(2)}) async-start(), calls=%async_computation.11 | async-start | bytes 8912896 | tf_op jit(solution)/shard_map/reduce_scatter | solution.py:235
  1808.0 675.9 %reduce-scatter.15.cloned.1.call-start = ((), (), s32[]{:S(2)}) async-start(), calls=%async_computation.10 | async-start | bytes 8912896 | tf_op jit(solution)/shard_map/reduce_scatter | solution.py:228
  (185 other events, 1766.7 us)
Sparse Core Ops, SparseCore 0:
  60.6 72.4 all-gather.7
  135.8 54.2 all-gather.5
  192.9 54.0 all-gather.9
  273.4 76.9 all-gather.11
  353.4 74.6 all-gather.13
  476.5 19.8 all-reduce.23
  507.6 55.3 all-gather.7
  565.7 54.3 all-gather.5
  622.8 54.0 all-gather.9
  703.5 76.9 all-gather.11
  783.5 74.6 all-gather.13
  906.6 19.8 all-reduce.23
  937.4 55.3 all-gather.7
  995.4 54.3 all-gather.5
  1052.6 54.0 all-gather.9
  1133.2 76.9 all-gather.11
  1213.4 74.6 all-gather.13
  1336.5 19.8 all-reduce.23
  1367.6 55.3 all-gather.7
  1425.6 54.3 all-gather.5
  1482.6 54.0 all-gather.9
  1563.2 76.9 all-gather.11
  1643.2 74.6 all-gather.13
  1766.3 19.8 all-reduce.23
  (8 shorter events, 148.9 us)
Sparse Core Ops, SparseCore 1:
  1797.2 72.1 reduce-scatter.12
  1872.1 77.2 reduce-scatter.10
  1952.1 77.8 reduce-scatter.6
  2032.8 77.5 reduce-scatter.8
  2113.3 187.5 reduce-scatter.16
  2303.7 180.1 reduce-scatter.14
